TPU v7x, 32 devices: a whole 2x2x4 slice. The times are simulated.
32 devices in a mesh: space: 8 (over y, x, core), member: 4 (over z).
Axes of the slice: x: 2, y: 2, z: 4, core: 2. Of those that a mesh axis runs over, the one named last changes fastest.
Arguments:
- obs_pert: bfloat16 [80, 16384], P('member', 'space'), may hold values from -6 to 6
- innovation: bfloat16 [16384], P('space'), may hold values from -6 to 6
- obs_prec: bfloat16 [16384], P('space'), may hold values from 1 to 100
- obs_lists: int32 [1536, 256], P('space'), may hold values from 0 to 6143
- loc_weight: bfloat16 [1536, 256], P('space'), may hold values from 0.049804688 to 1
- send_rows: int32 [8, 4, 8], P('space'), may hold values from 0 to 47
- ocean_src: int32 [48, 2], P('space'), may hold values from 0 to 31, as said below
- ocean_frac: float32 [48], P('space'), may hold values from 0 to 1
- ocean_ens: bfloat16 [80, 48, 2048], P(None, 'space', 'member'), may hold values from -6 to 6
Outputs:
- ocean_anal: bfloat16 [80, 48, 2048], P(None, 'space', 'member')
Inputs may be any that keep to these rules, and one draw needn't show every extreme that they name: `ocean_src`: the two slots of one ocean block differ.
All inputs are finite; a program needn't handle non-finite values.
Results may differ from a plain program's by a relative error of at most 0.0064.
Values may be sent and summed in bfloat16 or wider, within the bound.
A program may use at most 64 MiB of HBM per device.

v0:
```python
import jax
import jax.numpy as jnp
from jax import lax
from jax.sharding import PartitionSpec as P

ITERS = 12


def padded(cells, sides, width):
    for axis, dim in sides:
        count = lax.axis_size(axis)
        head = lax.slice_in_dim(cells, 0, width, axis=dim)
        tail = lax.slice_in_dim(cells, cells.shape[dim] - width, cells.shape[dim], axis=dim)
        cells = jnp.concatenate(
            [
                lax.ppermute(tail, axis, [(i, (i + 1) % count) for i in range(count)]),
                cells,
                lax.ppermute(head, axis, [((i + 1) % count, i) for i in range(count)]),
            ],
            axis=dim,
        )
    return cells


def transform(local_obs, loc_sel, innov_sel, prec_sel):
    members = local_obs.shape[0]
    obs_f32 = local_obs.astype(jnp.float32)
    obs_weight = loc_sel.astype(jnp.float32) * prec_sel.astype(jnp.float32)
    weighted = obs_f32 * obs_weight[None]
    gram = jnp.einsum("ibl,jbl->bij", weighted, obs_f32, precision=lax.Precision.HIGHEST)
    pulled = jnp.einsum(
        "ibl,bl->bi", weighted, innov_sel.astype(jnp.float32), precision=lax.Precision.HIGHEST
    )
    identity = jnp.eye(members, dtype=jnp.float32)
    precision_mat = (members - 1.0) * identity + gram
    scale_sum = jnp.trace(precision_mat, axis1=1, axis2=2)
    root_start = precision_mat / scale_sum[:, None, None]
    inverse_start = jnp.broadcast_to(identity, precision_mat.shape)

    def newton(iteration, carry):
        root_iter, inverse_iter = carry
        correction = 1.5 * identity - 0.5 * jnp.einsum(
            "bij,bjk->bik", inverse_iter, root_iter, precision=lax.Precision.HIGHEST
        )
        root_next = jnp.einsum(
            "bij,bjk->bik", root_iter, correction, precision=lax.Precision.HIGHEST
        )
        inverse_next = jnp.einsum(
            "bij,bjk->bik", correction, inverse_iter, precision=lax.Precision.HIGHEST
        )
        return (root_next, inverse_next)

    root_iter, inverse_iter = lax.fori_loop(0, ITERS, newton, (root_start, inverse_start))
    spread = jnp.sqrt((members - 1.0) / scale_sum)[:, None, None] * inverse_iter
    half_way = jnp.einsum("bij,bj->bi", inverse_iter, pulled, precision=lax.Precision.HIGHEST)
    mean_weight = (
        jnp.einsum("bij,bj->bi", inverse_iter, half_way, precision=lax.Precision.HIGHEST)
        / scale_sum[:, None]
    )
    return (spread + mean_weight[:, :, None]).astype(jnp.bfloat16)


def mix_pair(trans_one, trans_two, frac):
    frac_col = frac[:, None, None]
    return (
        (1.0 - frac_col) * trans_one.astype(jnp.float32) + frac_col * trans_two.astype(jnp.float32)
    ).astype(jnp.bfloat16)


def apply_weights(ensemble, mixed):
    ens_mean = jnp.mean(ensemble, axis=0, dtype=jnp.float32)
    deviation = (ensemble.astype(jnp.float32) - ens_mean[None]).astype(jnp.bfloat16)
    product = jnp.einsum("jol,oji->iol", deviation, mixed, preferred_element_type=jnp.float32)
    return (ens_mean[None] + product).astype(jnp.bfloat16)


def shards(
    obs_pert,
    innovation,
    obs_prec,
    obs_lists,
    loc_weight,
    send_rows,
    ocean_src,
    ocean_frac,
    ocean_ens,
):
    n_member = lax.axis_size("member")
    member_idx = lax.axis_index("member")
    tile_obs = obs_pert.shape[1]
    stacked = jnp.stack([innovation, obs_prec])
    pert_rim, info_rim = (
        padded(obs_pert, (("space", 1),), tile_obs),
        padded(stacked, (("space", 1),), tile_obs),
    )
    blocks = obs_lists.shape[0]
    group_len = blocks // n_member
    lists_mine = lax.dynamic_slice_in_dim(obs_lists, member_idx * group_len, group_len, 0)
    loc_mine = lax.dynamic_slice_in_dim(loc_weight, member_idx * group_len, group_len, 0)
    all_members = lax.all_gather(pert_rim, "member", axis=0, tiled=True)
    local_obs = all_members[:, lists_mine]
    innov_sel = info_rim[0][lists_mine]
    prec_sel = info_rim[1][lists_mine]
    weights = transform(local_obs, loc_mine, innov_sel, prec_sel)
    row_choice = lax.dynamic_index_in_dim(send_rows[0], member_idx, 0, keepdims=False)
    picked = weights[row_choice]
    arrived = lax.all_to_all(picked, "space", split_axis=0, concat_axis=0, tiled=True)
    weight_table = lax.all_gather(arrived, "member", axis=0, tiled=True)
    mixed = mix_pair(weight_table[ocean_src[:, 0]], weight_table[ocean_src[:, 1]], ocean_frac)
    return apply_weights(ocean_ens, mixed)


def solution(mesh):
    return jax.shard_map(
        shards,
        mesh=mesh,
        in_specs=(
            P("member", "space"),
            P("space"),
            P("space"),
            P("space", None),
            P("space", None),
            P("space", None, None),
            P("space", None),
            P("space"),
            P(None, "space", "member"),
        ),
        out_specs=P(None, "space", "member"),
        check_vma=False,
    )
```

profile of v0, /device:TPU:0, one launch (start us, length us, event | category | flops | bytes accessed | tf_op | source)
XLA Modules:
  0.0 422.7 jit_solution(8661184067395524443)
XLA Ops:
  1.4 3.4 collective-permute-start.3
  11.9 75.8 %gather_fusion.1 = bf16[12288]{0:T(1024)(128)(2,1)S(1)} fusion(bf16[6144]{0:T(1024)(128)(2,1)S(1)} %get-tuple-element.46, s32[12288]{0:T(1024)S(1)} %broadcast_clamp_fusion), kind=kCustom, calls=%fused_computation.1 | custom fusion | bytes 98304 | tf_op jit(solution)/shard_map/gather | solution.py:103
  88.5 75.8 %gather_fusion.2 = bf16[12288]{0:T(1024)(128)(2,1)S(1)} fusion(bf16[6144]{0:T(1024)(128)(2,1)S(1)} %get-tuple-element.45, s32[12288]{0:T(1024)S(1)} %broadcast_clamp_fusion), kind=kCustom, calls=%fused_computation.2 | custom fusion | bytes 98304 | tf_op jit(solution)/shard_map/gather | solution.py:102
  164.4 24.2 %all-gather = bf16[4,20,6144]{2,1,0:T(8,128)(2,1)S(1)} all-gather(bf16[1,20,6144]{2,1,0:T(8,128)(2,1)S(1)} %maximum_bitcast_fusion), channel_id=1, replica_groups=mesh['space'=8,'member'=4] {'member'}, dimensions={0}, use_global_device_ids=true | all-gather | bytes 1228800 | tf_op jit(solution)/shard_map/all_gather | solution.py:100
  189.7 43.6 %gather_fusion = bf16[12288,80]{1,0:T(8,128)(2,1)} fusion(bf16[80,6144]{0,1:T(8,128)(2,1)S(1)} %copy.27, s32[12288]{0:T(1024)S(1)} %broadcast_clamp_fusion), kind=kCustom, calls=%fused_computation | custom fusion | bytes 3981312 | tf_op jit(solution)/shard_map/gather | solution.py:101
  243.1 143.0 %while.13 = (s32[]{:T(128)}, f32[48,80,80]{1,2,0:T(8,128)}, f32[48,80,80]{2,1,0:T(8,128)S(1)}, s32[]{:T(128)}) while((s32[]{:T(128)}, f32[48,80,80]{1,2,0:T(8,128)}, f32[48,80,80]{2,1,0:T(8,128)S(1)}, s32[]{:T(128)}) %tuple.28), condition=%wide.region_3.4_spmd.clone, body=%wide.region_2.3_spmd.clone.sunk | while | flops 885977600 | bytes 16051253 | solution.py:53
  245.0 3.2 fusion.56
  250.5 4.7 %fusion.58 = f32[48,80,80]{1,2,0:T(8,128)} fusion(f32[48,80,80]{1,2,0:T(8,128)S(1)} %copy.54, f32[48,80,80]{2,1,0:T(8,128)S(1)} %fusion.56, f32[80,80]{1,0:T(8,128)S(1)} %fusion.57), kind=kOutput, calls=%fused_computation.10.clone.1 | convolution fusion | flops 295526400 | bytes 3712000 | tf_op jit(solution)/shard_map/while/body/eval_jaxpr/bij,bjk->bik/dot_general | solution.py:45
  256.9 3.2 fusion.56
  262.4 4.7 %fusion.58 = f32[48,80,80]{1,2,0:T(8,128)} fusion(f32[48,80,80]{1,2,0:T(8,128)S(1)} %copy.54, f32[48,80,80]{2,1,0:T(8,128)S(1)} %fusion.56, f32[80,80]{1,0:T(8,128)S(1)} %fusion.57), kind=kOutput, calls=%fused_computation.10.clone.1 | convolution fusion | flops 295526400 | bytes 3712000 | tf_op jit(solution)/shard_map/while/body/eval_jaxpr/bij,bjk->bik/dot_general | solution.py:45
  274.3 4.7 %fusion.58 = f32[48,80,80]{1,2,0:T(8,128)} fusion(f32[48,80,80]{1,2,0:T(8,128)S(1)} %copy.54, f32[48,80,80]{2,1,0:T(8,128)S(1)} %fusion.56, f32[80,80]{1,0:T(8,128)S(1)} %fusion.57), kind=kOutput, calls=%fused_computation.10.clone.1 | convolution fusion | flops 295526400 | bytes 3712000 | tf_op jit(solution)/shard_map/while/body/eval_jaxpr/bij,bjk->bik/dot_general | solution.py:45
  280.7 3.2 fusion.56
  286.2 4.7 %fusion.58 = f32[48,80,80]{1,2,0:T(8,128)} fusion(f32[48,80,80]{1,2,0:T(8,128)S(1)} %copy.54, f32[48,80,80]{2,1,0:T(8,128)S(1)} %fusion.56, f32[80,80]{1,0:T(8,128)S(1)} %fusion.57), kind=kOutput, calls=%fused_computation.10.clone.1 | convolution fusion | flops 295526400 | bytes 3712000 | tf_op jit(solution)/shard_map/while/body/eval_jaxpr/bij,bjk->bik/dot_general | solution.py:45
  292.6 3.2 fusion.56
  298.1 4.7 %fusion.58 = f32[48,80,80]{1,2,0:T(8,128)} fusion(f32[48,80,80]{1,2,0:T(8,128)S(1)} %copy.54, f32[48,80,80]{2,1,0:T(8,128)S(1)} %fusion.56, f32[80,80]{1,0:T(8,128)S(1)} %fusion.57), kind=kOutput, calls=%fused_computation.10.clone.1 | convolution fusion | flops 295526400 | bytes 3712000 | tf_op jit(solution)/shard_map/while/body/eval_jaxpr/bij,bjk->bik/dot_general | solution.py:45
  304.5 3.2 fusion.56
  310.0 4.7 %fusion.58 = f32[48,80,80]{1,2,0:T(8,128)} fusion(f32[48,80,80]{1,2,0:T(8,128)S(1)} %copy.54, f32[48,80,80]{2,1,0:T(8,128)S(1)} %fusion.56, f32[80,80]{1,0:T(8,128)S(1)} %fusion.57), kind=kOutput, calls=%fused_computation.10.clone.1 | convolution fusion | flops 295526400 | bytes 3712000 | tf_op jit(solution)/shard_map/while/body/eval_jaxpr/bij,bjk->bik/dot_general | solution.py:45
  316.4 3.2 fusion.56
  321.9 4.7 %fusion.58 = f32[48,80,80]{1,2,0:T(8,128)} fusion(f32[48,80,80]{1,2,0:T(8,128)S(1)} %copy.54, f32[48,80,80]{2,1,0:T(8,128)S(1)} %fusion.56, f32[80,80]{1,0:T(8,128)S(1)} %fusion.57), kind=kOutput, calls=%fused_computation.10.clone.1 | convolution fusion | flops 295526400 | bytes 3712000 | tf_op jit(solution)/shard_map/while/body/eval_jaxpr/bij,bjk->bik/dot_general | solution.py:45
  328.3 3.2 fusion.56
  333.8 4.7 %fusion.58 = f32[48,80,80]{1,2,0:T(8,128)} fusion(f32[48,80,80]{1,2,0:T(8,128)S(1)} %copy.54, f32[48,80,80]{2,1,0:T(8,128)S(1)} %fusion.56, f32[80,80]{1,0:T(8,128)S(1)} %fusion.57), kind=kOutput, calls=%fused_computation.10.clone.1 | convolution fusion | flops 295526400 | bytes 3712000 | tf_op jit(solution)/shard_map/while/body/eval_jaxpr/bij,bjk->bik/dot_general | solution.py:45
  340.2 3.2 fusion.56
  345.7 4.7 %fusion.58 = f32[48,80,80]{1,2,0:T(8,128)} fusion(f32[48,80,80]{1,2,0:T(8,128)S(1)} %copy.54, f32[48,80,80]{2,1,0:T(8,128)S(1)} %fusion.56, f32[80,80]{1,0:T(8,128)S(1)} %fusion.57), kind=kOutput, calls=%fused_computation.10.clone.1 | convolution fusion | flops 295526400 | bytes 3712000 | tf_op jit(solution)/shard_map/while/body/eval_jaxpr/bij,bjk->bik/dot_general | solution.py:45
  352.1 3.2 fusion.56
  357.6 4.7 %fusion.58 = f32[48,80,80]{1,2,0:T(8,128)} fusion(f32[48,80,80]{1,2,0:T(8,128)S(1)} %copy.54, f32[48,80,80]{2,1,0:T(8,128)S(1)} %fusion.56, f32[80,80]{1,0:T(8,128)S(1)} %fusion.57), kind=kOutput, calls=%fused_computation.10.clone.1 | convolution fusion | flops 295526400 | bytes 3712000 | tf_op jit(solution)/shard_map/while/body/eval_jaxpr/bij,bjk->bik/dot_general | solution.py:45
  364.0 3.2 fusion.56
  369.5 4.7 %fusion.58 = f32[48,80,80]{1,2,0:T(8,128)} fusion(f32[48,80,80]{1,2,0:T(8,128)S(1)} %copy.54, f32[48,80,80]{2,1,0:T(8,128)S(1)} %fusion.56, f32[80,80]{1,0:T(8,128)S(1)} %fusion.57), kind=kOutput, calls=%fused_computation.10.clone.1 | convolution fusion | flops 295526400 | bytes 3712000 | tf_op jit(solution)/shard_map/while/body/eval_jaxpr/bij,bjk->bik/dot_general | solution.py:45
  375.9 3.2 fusion.56
  381.4 4.7 %fusion.58 = f32[48,80,80]{1,2,0:T(8,128)} fusion(f32[48,80,80]{1,2,0:T(8,128)S(1)} %copy.54, f32[48,80,80]{2,1,0:T(8,128)S(1)} %fusion.56, f32[80,80]{1,0:T(8,128)S(1)} %fusion.57), kind=kOutput, calls=%fused_computation.10.clone.1 | convolution fusion | flops 295526400 | bytes 3712000 | tf_op jit(solution)/shard_map/while/body/eval_jaxpr/bij,bjk->bik/dot_general | solution.py:45
  394.5 3.4 all-to-all-start
  397.9 5.8 %all-to-all-done = bf16[8,80,80]{2,1,0:T(8,128)(2,1)S(1)} async-done(((bf16[8,80,80]{2,1,0:T(8,128)(2,1)}), bf16[8,80,80]{2,1,0:T(8,128)(2,1)S(1)}, u32[]{:S(2)}, u32[]{:S(2)}) %all-to-all-start) | async-done | bytes 102432 | tf_op jit(solution)/shard_map/all_to_all | solution.py:107
  403.7 16.6 %all_gather.7 = bf16[32,80,80]{2,1,0:T(8,128)(2,1)S(1)} all-gather(bf16[8,80,80]{2,1,0:T(8,128)(2,1)S(1)} %all-to-all-done), channel_id=1, replica_groups=mesh['space'=8,'member'=4] {'member'}, dimensions={0}, use_global_device_ids=true | all-gather | bytes 512000 | tf_op jit(solution)/shard_map/all_gather | solution.py:108
  (101 shorter events, 81.5 us)
Async XLA Ops:
  1.4 10.2 %collective-permute-start.3 = (bf16[2,2048]{1,0:T(2,128)(2,1)S(1)}, bf16[2,2048]{1,0:T(2,128)(2,1)S(1)}, u32[]{:S(2)}, u32[]{:S(2)}) collective-permute-start(bf16[2,2048]{1,0:T(2,128)(2,1)S(1)} %pad_maximum_fusion.1), channel_id=1, source_target_pairs={{4,0},{8,4},{12,8},{16,12},{20,16},{24,20},{28,24},{0,28},{5,1},{9... | collective-permute-start | bytes 24584 | tf_op jit(solution)/shard_map/ppermute | solution.py:18
  4.8 6.8 %collective-permute-start.2 = (bf16[2,2048]{1,0:T(2,128)(2,1)S(1)}, bf16[2,2048]{1,0:T(2,128)(2,1)S(1)}, u32[]{:S(2)}, u32[]{:S(2)}) collective-permute-start(bf16[2,2048]{1,0:T(2,128)(2,1)S(1)} %pad_maximum_fusion.1), channel_id=1, source_target_pairs={{0,4},{4,8},{8,12},{12,16},{16,20},{20,24},{24,28},{28,0},{1,5},{5... | collective-permute-start | bytes 24584 | tf_op jit(solution)/shard_map/ppermute | solution.py:16
  4.8 159.5 %collective-permute-start = (bf16[20,2048]{1,0:T(8,128)(2,1)}, bf16[20,2048]{1,0:T(8,128)(2,1)S(1)}, u32[]{:S(2)}, u32[]{:S(2)}) collective-permute-start(bf16[20,2048]{1,0:T(8,128)(2,1)} %param.11), channel_id=1, source_target_pairs={{0,4},{4,8},{8,12},{12,16},{16,20},{20,24},{24,28},{28,0},{1,5},{5... | collective-permute-start | bytes 245768 | tf_op jit(solution)/shard_map/ppermute | solution.py:16
  4.8 159.5 %collective-permute-start.1 = (bf16[20,2048]{1,0:T(8,128)(2,1)}, bf16[20,2048]{1,0:T(8,128)(2,1)S(1)}, u32[]{:S(2)}, u32[]{:S(2)}) collective-permute-start(bf16[20,2048]{1,0:T(8,128)(2,1)} %param.11), channel_id=1, source_target_pairs={{4,0},{8,4},{12,8},{16,12},{20,16},{24,20},{28,24},{0,28},{5,1},{9... | collective-permute-start | bytes 245768 | tf_op jit(solution)/shard_map/ppermute | solution.py:18
  88.5 75.9 %copy-start.1 = (bf16[20,2048]{1,0:T(8,128)(2,1)S(1)}, bf16[20,2048]{1,0:T(8,128)(2,1)}, u32[]{:S(2)}) copy-start(bf16[20,2048]{1,0:T(8,128)(2,1)} %param.11) | copy-start | bytes 245764
  392.5 28.9 %copy-start = (bf16[80,6,512]{2,0,1:T(8,128)(2,1)S(1)}, bf16[80,6,512]{2,0,1:T(8,128)(2,1)}, u32[]{:S(2)}) copy-start(bf16[80,6,512]{2,0,1:T(8,128)(2,1)} %param.19) | copy-start | bytes 1474564
  392.5 28.9 %copy-start.2 = (f32[6]{0:T(128)S(1)}, f32[6]{0:T(128)}, u32[]{:S(2)}) copy-start(f32[6]{0:T(128)} %param.18) | copy-start | bytes 76
  394.5 9.2 %all-to-all-start = ((bf16[8,80,80]{2,1,0:T(8,128)(2,1)}), bf16[8,80,80]{2,1,0:T(8,128)(2,1)S(1)}, u32[]{:S(2)}, u32[]{:S(2)}) async-start(bf16[8,80,80]{2,1,0:T(8,128)(2,1)} %gather_fusion.3), calls=%async_computation | async-start | bytes 327680 | tf_op jit(solution)/shard_map/all_to_all | solution.py:107
where the time goes:
time: 424 us; the launch traced here: 423 us
  local copies, waits for them, and re-layouts  225 us (53%)
  matrix products  134 us (32%)
  blocking collectives  40.8 us (10%)
  starting transfers between devices  9.46 us (2%)
  other arithmetic  6.15 us (1%)
  waiting for transfers between devices  5.78 us (1%)
    gather x2, local copies, waits for them, and re-layouts, shards(): innov_sel = info_rim[0][lists_mine]  75.8 us
    gather x1, local copies, waits for them, and re-layouts, shards(): prec_sel = info_rim[1][lists_mine]  75.8 us
    dot_general x12, matrix products, newton(): jnp.einsum('bij,bjk->bik', root_iter, correction, precision=lax.Precision...  56.2 us
    gather x2, local copies, waits for them, and re-layouts, shards(): local_obs = all_members[:, lists_mine]  46.7 us
    dot_general x12, matrix products, newton(): jnp.einsum('bij,bjk->bik', inverse_iter, root_iter, precision=lax.Precisi...  38.9 us
    dot_general x12, matrix products, newton(): jnp.einsum('bij,bjk->bik', correction, inverse_iter, precision=lax.Precis...  27.3 us
    all_gather x1, blocking collectives, shards(): all_members = lax.all_gather(pert_rim, 'member', axis=0, tiled=True)  24.2 us
    while x24, local copies, waits for them, and re-layouts  20.1 us
  transfers between devices with their start and end apart: 5, of which 1 were waited for; matrix products, arithmetic and copies ran while one was open for 37% of the time, Pallas kernels for 0%

commit v1 on v0

v1 whole, which is shorter than its diff:
```python
import functools

import jax
import jax.numpy as jnp
from jax import lax
from jax.experimental import pallas as pl
from jax.experimental.pallas import tpu as pltpu
from jax.sharding import PartitionSpec as P

ITERS = 12
LANES = 128
CHUNK = 512


def split(value):
    high = value.astype(jnp.bfloat16)
    low = (value - high.astype(jnp.float32)).astype(jnp.bfloat16)
    return high, low


def left_side(value):
    return jnp.concatenate(split(value), axis=1)


def right_side(value):
    pair = left_side(value)
    filler = jnp.zeros((LANES - pair.shape[0], pair.shape[1]), jnp.bfloat16)
    return jnp.concatenate([pair, filler, pair, filler], axis=0)


def halves(product):
    return product[:, :LANES] + product[:, LANES:]


def mm(lhs, rhs):
    return jnp.dot(lhs, rhs, preferred_element_type=jnp.float32)


def transform_kernel(
    group, members, send_ref, lists_ref, loc_ref, left_ref, mid_ref, right_ref, prec_ref, out_ref,
    loc_f32, dense, gram, root, inverse, pulled, scales,
):
    member_idx = lax.axis_index("member")
    n_member = send_ref.shape[0]
    group_len = lists_ref.shape[0] // n_member
    first = pl.program_id(0) * group
    loc_f32[...] = loc_ref[...].astype(jnp.float32)
    his = dense.shape[1]
    lobs = lists_ref.shape[1]
    hi_iota = lax.broadcasted_iota(jnp.int32, (his, lobs), 0)
    lo_iota = lax.broadcasted_iota(jnp.int32, (LANES, lobs), 0)
    for b in range(group):
        row = send_ref[member_idx, first + b] + member_idx * group_len
        spots = lists_ref[pl.ds(row, 1), :]
        taper = loc_f32[pl.ds(row, 1), :]
        hi_hot = jnp.where(hi_iota == spots // LANES, taper, 0.0).astype(jnp.bfloat16)
        lo_hot = jnp.where(lo_iota == spots % LANES, 1.0, 0.0).astype(jnp.bfloat16)
        dense[b] = prec_ref[...] * lax.dot_general(
            hi_hot, lo_hot, (((1,), (1,)), ((), ())), preferred_element_type=jnp.float32
        )
    gram[...] = jnp.zeros_like(gram)
    per = CHUNK // LANES
    for piece, ref in enumerate((left_ref, mid_ref, right_ref)):
        tile_obs = ref.shape[1]

        def chunk_step(c, carry, ref=ref, base=piece * (tile_obs // LANES)):
            cells = ref[:, pl.ds(pl.multiple_of(c * CHUNK, CHUNK), CHUNK)]
            wide = cells[:members].astype(jnp.float32)
            highs, lows = [], []
            for b in range(group):
                parts = []
                for j in range(per):
                    weight = dense[b, pl.ds(base + c * per + j, 1), :]
                    parts.append(wide[:, j * LANES : (j + 1) * LANES] * weight)
                high, low = split(jnp.concatenate(parts, axis=1))
                highs.append(high)
                lows.append(low)
            rhs = (((1,), (1,)), ((), ()))
            for b in range(group):
                both = lax.dot_general(
                    highs[b], cells, rhs, preferred_element_type=jnp.float32
                ) + lax.dot_general(lows[b], cells, rhs, preferred_element_type=jnp.float32)
                gram[b, :, : cells.shape[0]] += both
            return carry

        lax.fori_loop(0, tile_obs // CHUNK, chunk_step, 0)

    rows = lax.broadcasted_iota(jnp.int32, (members, LANES), 0)
    cols = lax.broadcasted_iota(jnp.int32, (members, LANES), 1)
    on_diag = rows == cols
    half3 = jnp.where(on_diag, 1.5, 0.0)
    for b in range(group):
        both = gram[b]
        pulled[b] = jnp.sum(jnp.where(cols == members, both, 0.0), axis=1, keepdims=True)
        matrix = jnp.where(cols < members, both, 0.0) + jnp.where(on_diag, members - 1.0, 0.0)
        scale = jnp.sum(
            jnp.sum(jnp.where(on_diag, matrix, 0.0), axis=1, keepdims=True), axis=0, keepdims=True
        )
        scales[b] = jnp.broadcast_to(scale, (1, LANES))
        start = matrix / scale
        correction = half3 - 0.5 * start
        root[b] = halves(mm(left_side(start), right_side(correction)))
        inverse[b] = correction

    def newton(step, carry):
        corrections = []
        roots, inverses = [], []
        for b in range(group):
            roots.append(left_side(root[b]))
            inverses.append(left_side(inverse[b]))
            filler = jnp.zeros((LANES - members, 2 * LANES), jnp.bfloat16)
            rhs = jnp.concatenate([roots[b], filler, roots[b], filler], axis=0)
            corrections.append(half3 - 0.5 * halves(mm(inverses[b], rhs)))
        for b in range(group):
            both = halves(
                mm(jnp.concatenate([roots[b], inverses[b]], axis=0), right_side(corrections[b]))
            )
            root[b] = both[:members]
            inverse[b] = both[members:]
        return carry

    lax.fori_loop(0, ITERS - 1, newton, 0)

    for b in range(group):
        z = inverse[b]
        scale = scales[b]
        half_way = jnp.sum(z * pulled[b], axis=0, keepdims=True)
        mean_weight = jnp.sum(z * half_way, axis=1, keepdims=True) / scale[:, :1]
        trans = jnp.sqrt((members - 1.0) / scale) * z + mean_weight
        out_ref[b] = trans[:, :members].astype(jnp.bfloat16)


def transforms(send, lists, loc, left, mid, right, prec, count):
    members = left.shape[0] - 16
    group = 8 if count % 8 == 0 else count
    his = prec.shape[0]
    full = lambda a: pl.BlockSpec(a.shape, lambda i, n=a.ndim: (0,) * n)
    return pl.pallas_call(
        functools.partial(transform_kernel, group, members),
        grid=(count // group,),
        in_specs=[pl.BlockSpec(memory_space=pltpu.SMEM)]
        + [full(a) for a in (lists, loc, left, mid, right, prec)],
        out_specs=pl.BlockSpec((group, members, members), lambda i: (i, 0, 0)),
        out_shape=jax.ShapeDtypeStruct((count, members, members), jnp.bfloat16),
        scratch_shapes=[
            pltpu.VMEM(loc.shape, jnp.float32),
            pltpu.VMEM((group, his, LANES), jnp.float32),
            pltpu.VMEM((group, members, LANES), jnp.float32),
            pltpu.VMEM((group, members, LANES), jnp.float32),
            pltpu.VMEM((group, members, LANES), jnp.float32),
            pltpu.VMEM((group, members, 1), jnp.float32),
            pltpu.VMEM((group, 1, LANES), jnp.float32),
        ],
        name="transforms",
    )(send, lists, loc, left, mid, right, prec)


def shift(cells, by):
    count = lax.axis_size("space")
    return lax.ppermute(cells, "space", [(i, (i + by) % count) for i in range(count)])


def mix_pair(trans_one, trans_two, frac):
    frac_col = frac[:, None, None]
    return (
        (1.0 - frac_col) * trans_one.astype(jnp.float32) + frac_col * trans_two.astype(jnp.float32)
    ).astype(jnp.bfloat16)


def apply_weights(ensemble, mixed):
    ens_mean = jnp.mean(ensemble, axis=0, dtype=jnp.float32)
    deviation = (ensemble.astype(jnp.float32) - ens_mean[None]).astype(jnp.bfloat16)
    product = jnp.einsum("jol,oji->iol", deviation, mixed, preferred_element_type=jnp.float32)
    return (ens_mean[None] + product).astype(jnp.bfloat16)


def shards(
    obs_pert,
    innovation,
    obs_prec,
    obs_lists,
    loc_weight,
    send_rows,
    ocean_src,
    ocean_frac,
    ocean_ens,
):
    n_space = lax.axis_size("space")
    tile_obs = obs_pert.shape[1]
    members = lax.all_gather(obs_pert, "member", axis=0, tiled=True)
    extra = jnp.zeros((16, tile_obs), jnp.bfloat16).at[0].set(innovation).at[1].set(obs_prec)
    mid = jnp.concatenate([members, extra], axis=0)
    left, right = shift(mid, 1), shift(mid, -1)
    k = members.shape[0]
    prec = jnp.stack([left[k + 1], obs_prec, right[k + 1]]).astype(jnp.float32)
    prec = prec.reshape(-1, LANES)
    weights = transforms(send_rows[0], obs_lists, loc_weight, left, mid, right, prec, n_space)
    arrived = lax.all_to_all(weights, "space", split_axis=0, concat_axis=0, tiled=True)
    weight_table = lax.all_gather(arrived, "member", axis=0, tiled=True)
    mixed = mix_pair(weight_table[ocean_src[:, 0]], weight_table[ocean_src[:, 1]], ocean_frac)
    return apply_weights(ocean_ens, mixed)


def solution(mesh):
    return jax.shard_map(
        shards,
        mesh=mesh,
        in_specs=(
            P("member", "space"),
            P("space"),
            P("space"),
            P("space", None),
            P("space", None),
            P("space", None, None),
            P("space", None),
            P("space"),
            P(None, "space", "member"),
        ),
        out_specs=P(None, "space", "member"),
        check_vma=False,
    )
```

time: 424 us -> 76.6 us (0.18)
  local copies, waits for them, and re-layouts: 225 us -> 2.88 us
  matrix products: 134 us -> 1.2 us
  Pallas kernels: 0 us -> 16.7 us
  waiting for transfers between devices: 5.78 us -> 13.5 us
  blocking collectives: 40.8 us -> 34.8 us
  other arithmetic: 6.15 us -> 0.17 us
    gather x6 -> x0, local copies, waits for them, and re-layouts: 200 us -> none  [the longest x2 75.8 us: shards(): innov_sel = info_rim[0][lists_mine]]
    dot_general x40 -> x0, matrix products: 133 us -> none  [the longest x12 56.2 us: newton(): jnp.einsum('bij,bjk->bik', root_iter, correction, precision=lax.Precision...]
    while x24 -> x0, local copies, waits for them, and re-layouts: 20.1 us -> none
    pallas_call x0 -> x1, Pallas kernels: none -> 16.7 us  [transforms(): pl.pallas_call(functools.partial(transform_kernel, group, members), grid=...]
    all_gather x1, blocking collectives: 24.2 us -> 16.5 us  [shards(): members = lax.all_gather(obs_pert, 'member', axis=0, tiled=True)]
    ppermute x4 -> x2, waiting for transfers between devices: 0.01 us -> 7.69 us  [shift(): lax.ppermute(cells, 'space', [(i, (i + by) % count) for i in range(count)])]
  transfers between devices with their start and end apart: 5 -> 3, of which waited for: 1 -> 2; matrix products, arithmetic and copies ran while one was open for 37% -> 0% of each run, Pallas kernels for 0% -> 0%
where the time goes in v1:
time: 76.6 us; the launch traced here: 76.2 us
  blocking collectives  34.8 us (45%)
  Pallas kernels  16.7 us (22%)
  waiting for transfers between devices  13.5 us (18%)
  starting transfers between devices  6.75 us (9%)
  local copies, waits for them, and re-layouts  2.88 us (4%)
  matrix products  1.2 us (2%)
    all_gather x1, blocking collectives, shards(): weight_table = lax.all_gather(arrived, 'member', axis=0, tiled=True)  18.4 us
    pallas_call x1, Pallas kernels, transforms(): pl.pallas_call(functools.partial(transform_kernel, group, members), grid=...  16.7 us
    all_gather x1, blocking collectives, shards(): members = lax.all_gather(obs_pert, 'member', axis=0, tiled=True)  16.5 us
    ppermute x2, waiting for transfers between devices, shift(): lax.ppermute(cells, 'space', [(i, (i + by) % count) for i in range(count)])  7.69 us
    all_to_all x1, waiting for transfers between devices, shards(): lax.all_to_all(weights, 'space', split_axis=0, concat_axis=0, tiled=True)  5.84 us
    all_to_all x1, starting transfers between devices, shards(): lax.all_to_all(weights, 'space', split_axis=0, concat_axis=0, tiled=True)  4.06 us
    ppermute x2, starting transfers between devices, shift(): lax.ppermute(cells, 'space', [(i, (i + by) % count) for i in range(count)])  2.69 us
  transfers between devices with their start and end apart: 3, of which 2 were waited for; matrix products, arithmetic and copies ran while one was open for 0% of the time, Pallas kernels for 0%

profile of v1, /device:TPU:0, one launch (start us, length us, event | category | flops | bytes accessed | tf_op | source)
XLA Modules:
  0.0 76.2 jit_solution(13491493155996951001)
XLA Ops:
  0.0 0.0 copy-start.4
  0.0 0.7 reshape.63
  0.7 0.0 copy-done.4
  0.7 16.5 %all-gather = bf16[4,20,2048]{2,1,0:T(8,128)(2,1)S(1)} all-gather(bf16[1,20,2048]{2,1,0:T(8,128)(2,1)} %bitcast.8), channel_id=1, replica_groups=mesh['space'=8,'member'=4] {'member'}, dimensions={0}, use_global_device_ids=true | all-gather | bytes 409600 | tf_op jit(solution)/shard_map/all_gather | solution.py:190
  17.2 0.1 reshape.82
  17.3 0.0 copy-start
  17.3 0.1 scatter.9
  17.4 0.0 copy-start.5
  17.5 0.0 copy-start.1
  17.5 0.0 copy-start.6
  17.5 0.1 collective-permute-start
  17.6 2.6 %collective-permute-start.1 = (bf16[96,2048]{1,0:T(8,128)(2,1)S(1)}, bf16[96,2048]{1,0:T(8,128)(2,1)S(1)}, u32[]{:S(2)}, u32[]{:S(2)}) collective-permute-start(bf16[96,2048]{1,0:T(8,128)(2,1)S(1)} %pad_maximum_fusion.mid_ref), channel_id=1, source_target_pairs={{0,28},{4,0},{8,4},{12,8},{16,12},{20,16},{24,20},{28,24},{1,29},{... | collective-permute-start | bytes 1179656 | tf_op jit(solution)/shard_map/ppermute | solution.py:160
  20.2 0.0 copy-done.5
  20.2 0.0 copy-done.6
  20.2 0.0 copy-done
  20.2 0.1 convert_reduce_fusion
  20.3 7.7 %collective-permute-done.left_ref = bf16[96,2048]{1,0:T(8,128)(2,1)S(1)} collective-permute-done((bf16[96,2048]{1,0:T(8,128)(2,1)S(1)}, bf16[96,2048]{1,0:T(8,128)(2,1)S(1)}, u32[]{:S(2)}, u32[]{:S(2)}) %collective-permute-start) | collective-permute-done | bytes 393248 | tf_op jit(solution)/shard_map/ppermute | solution.py:160
  28.0 0.0 copy-start.2
  28.1 0.0 collective-permute-done.1.right_ref
  28.1 0.0 copy-start.3
  28.1 0.8 %reshape.64.prec_ref = f32[48,128]{1,0:T(8,128)} reshape(f32[3,2048]{1,0:T(4,128)S(1)} %maximum_convert_fusion) | data formatting | bytes 49152 | tf_op jit(solution)/shard_map/convert_element_type | solution.py:195
  28.9 0.0 copy-done.1
  28.9 0.0 copy-done.2
  28.9 0.0 copy-done.3
  28.9 16.7 %transforms.1 = bf16[8,80,80]{2,1,0:T(8,128)(2,1)} custom-call(s32[4,8]{1,0:T(4,128)} %bitcast.9, s32[192,256]{1,0:T(8,128)} %lists_ref.1, bf16[192,256]{1,0:T(8,128)(2,1)} %loc_ref.1, bf16[96,2048]{1,0:T(8,128)(2,1)} %copy-done.2, bf16[96,2048]{1,0:T(8,128)(2,1)} %copy-done.1, bf16[96,2048]{1,0:T(8,128)(2,1)} %copy-done.3, f32[48,128]{1,0:T(8,128)} %reshape.64.prec_ref), custom_call_target="tpu_custom_call" | custom-call | tf_op jit(solution)/shard_map/transforms/pallas_call | solution.py:138
  45.6 4.1 %all-to-all-start = ((bf16[8,80,80]{2,1,0:T(8,128)(2,1)}), bf16[8,80,80]{2,1,0:T(8,128)(2,1)S(1)}, u32[]{:S(2)}, u32[]{:S(2)}) async-start(bf16[8,80,80]{2,1,0:T(8,128)(2,1)} %transforms.1), calls=%async_computation | async-start | bytes 327680 | tf_op jit(solution)/shard_map/all_to_all | solution.py:198
  49.7 5.8 %all-to-all-done = bf16[8,80,80]{2,1,0:T(8,128)(2,1)S(1)} async-done(((bf16[8,80,80]{2,1,0:T(8,128)(2,1)}), bf16[8,80,80]{2,1,0:T(8,128)(2,1)S(1)}, u32[]{:S(2)}, u32[]{:S(2)}) %all-to-all-start) | async-done | bytes 102432 | tf_op jit(solution)/shard_map/all_to_all | solution.py:198
  55.5 18.4 %all_gather.7 = bf16[32,80,80]{2,1,0:T(8,128)(2,1)S(1)} all-gather(bf16[8,80,80]{2,1,0:T(8,128)(2,1)S(1)} %all-to-all-done), channel_id=1, replica_groups=mesh['space'=8,'member'=4] {'member'}, dimensions={0}, use_global_device_ids=true | all-gather | bytes 512000 | tf_op jit(solution)/shard_map/all_gather | solution.py:199
  73.9 0.6 gather_fusion
  74.5 0.6 gather_fusion.1
  75.0 1.2 %fusion.1 = bf16[80,6,512]{2,0,1:T(8,128)(2,1)} fusion(bf16[80,6,512]{2,0,1:T(8,128)(2,1)S(1)} %copy-done, f32[6,512]{1,0:T(8,128)S(1)} %broadcast_multiply_fusion, bf16[6,80,80]{2,1,0:T(8,128)(2,1)S(1)} %gather_fusion.1, bf16[6,80,80]{2,1,0:T(8,128)(2,1)S(1)} %gather_fusion, f32[6]{0:T(128)S(1)} %copy-done.6, f32[6]{0:T(128)S(1)} %broadcast_subtract_fusion), kind=kOutput, calls=%fused_computation.6 | convolution fusion | flops 40780800 | bytes 1148976 | tf_op jit(solution)/shard_map/jol,oji->iol/dot_general | solution.py:173
  (10 shorter events, 0.1 us)
Async XLA Ops:
  0.0 0.7 copy-start.4
  17.3 3.0 %copy-start = (bf16[80,6,512]{2,0,1:T(8,128)(2,1)S(1)}, bf16[80,6,512]{2,0,1:T(8,128)(2,1)}, u32[]{:S(2)}) copy-start(bf16[80,6,512]{2,0,1:T(8,128)(2,1)} %param.21) | copy-start | bytes 1474564
  17.4 2.8 %copy-start.5 = (s32[6,2]{0,1:T(2,128)S(1)}, s32[6,2]{0,1:T(2,128)}, u32[]{:S(2)}) copy-start(s32[6,2]{0,1:T(2,128)} %param.19) | copy-start | bytes 148
  17.5 11.4 %copy-start.1 = (bf16[96,2048]{1,0:T(8,128)(2,1)}, bf16[96,2048]{1,0:T(8,128)(2,1)S(1)}, u32[]{:S(2)}) copy-start(bf16[96,2048]{1,0:T(8,128)(2,1)S(1)} %pad_maximum_fusion.mid_ref) | copy-start | bytes 1179652
  17.5 2.7 %copy-start.6 = (f32[6]{0:T(128)S(1)}, f32[6]{0:T(128)}, u32[]{:S(2)}) copy-start(f32[6]{0:T(128)} %param.20) | copy-start | bytes 76
  17.5 10.5 %collective-permute-start = (bf16[96,2048]{1,0:T(8,128)(2,1)S(1)}, bf16[96,2048]{1,0:T(8,128)(2,1)S(1)}, u32[]{:S(2)}, u32[]{:S(2)}) collective-permute-start(bf16[96,2048]{1,0:T(8,128)(2,1)S(1)} %pad_maximum_fusion.mid_ref), channel_id=1, source_target_pairs={{0,4},{4,8},{8,12},{12,16},{16,20},{20,24},{24,28},{28,0},{1,5},{5... | collective-permute-start | bytes 1179656 | tf_op jit(solution)/shard_map/ppermute | solution.py:160
  17.6 10.5 %collective-permute-start.1 = (bf16[96,2048]{1,0:T(8,128)(2,1)S(1)}, bf16[96,2048]{1,0:T(8,128)(2,1)S(1)}, u32[]{:S(2)}, u32[]{:S(2)}) collective-permute-start(bf16[96,2048]{1,0:T(8,128)(2,1)S(1)} %pad_maximum_fusion.mid_ref), channel_id=1, source_target_pairs={{0,28},{4,0},{8,4},{12,8},{16,12},{20,16},{24,20},{28,24},{1,29},{... | collective-permute-start | bytes 1179656 | tf_op jit(solution)/shard_map/ppermute | solution.py:160
  28.0 0.9 %copy-start.2 = (bf16[96,2048]{1,0:T(8,128)(2,1)}, bf16[96,2048]{1,0:T(8,128)(2,1)S(1)}, u32[]{:S(2)}) copy-start(bf16[96,2048]{1,0:T(8,128)(2,1)S(1)} %collective-permute-done.left_ref) | copy-start | bytes 1179652
  28.1 0.8 %copy-start.3 = (bf16[96,2048]{1,0:T(8,128)(2,1)}, bf16[96,2048]{1,0:T(8,128)(2,1)S(1)}, u32[]{:S(2)}) copy-start(bf16[96,2048]{1,0:T(8,128)(2,1)S(1)} %collective-permute-done.1.right_ref) | copy-start | bytes 1179652
  45.6 9.9 %all-to-all-start = ((bf16[8,80,80]{2,1,0:T(8,128)(2,1)}), bf16[8,80,80]{2,1,0:T(8,128)(2,1)S(1)}, u32[]{:S(2)}, u32[]{:S(2)}) async-start(bf16[8,80,80]{2,1,0:T(8,128)(2,1)} %transforms.1), calls=%async_computation | async-start | bytes 327680 | tf_op jit(solution)/shard_map/all_to_all | solution.py:198

commit v2 on v1

v2 whole, which is shorter than its diff:
```python
import functools

import jax
import jax.numpy as jnp
from jax import lax
from jax.experimental import pallas as pl
from jax.experimental.pallas import tpu as pltpu
from jax.sharding import PartitionSpec as P

ITERS = 12
LANES = 128
CHUNK = 512


def split(value):
    high = value.astype(jnp.bfloat16)
    low = (value - high.astype(jnp.float32)).astype(jnp.bfloat16)
    return high, low


def left_side(value):
    return jnp.concatenate(split(value), axis=1)


def right_side(value):
    pair = left_side(value)
    filler = jnp.zeros((LANES - pair.shape[0], pair.shape[1]), jnp.bfloat16)
    return jnp.concatenate([pair, filler, pair, filler], axis=0)


def halves(product):
    return product[:, :LANES] + product[:, LANES:]


def mm(lhs, rhs):
    return jnp.dot(lhs, rhs, preferred_element_type=jnp.float32)


MESH = pl.DeviceIdType.MESH


def remote(src, dst, send_sem, recv_sem, device):
    return pltpu.make_async_remote_copy(
        src_ref=src, dst_ref=dst, send_sem=send_sem, recv_sem=recv_sem,
        device_id=device, device_id_type=MESH,
    )


def letkf_kernel(
    group, ns, nm,
    send_ref, coef_ref, lists_ref, loc_ref, pert_ref, extra_ref, out_ref,
    pert_all, extra_all, loc_f32, dense, gram, root, inverse, pulled, scales,
    trans_out, trans_in, up_out, up_in, down_out, down_in, mixed,
    z_send, z_recv, near_send, near_recv, info_send, info_recv, t_send, t_recv,
    up_send, up_recv, down_send, down_recv,
):
    s = lax.axis_index("space")
    m = lax.axis_index("member")
    members = pert_ref.shape[0] * nm
    tile_obs = pert_ref.shape[1]
    tile_his = tile_obs // LANES
    group_len = lists_ref.shape[0] // nm
    oblocks = out_ref.shape[0]
    z_peers = [lax.rem(m + k, nm) for k in range(1, nm)]
    s_peers = [lax.rem(s + k, ns) for k in range(1, ns)]
    left, right = lax.rem(s + ns - 1, ns), lax.rem(s + 1, ns)

    barrier = pltpu.get_barrier_semaphore()
    for peer in z_peers:
        pl.semaphore_signal(barrier, inc=1, device_id=(s, peer), device_id_type=MESH)
    for peer in s_peers:
        pl.semaphore_signal(barrier, inc=1, device_id=(peer, m), device_id_type=MESH)
    pl.semaphore_wait(barrier, len(z_peers) + len(s_peers))

    def to_z(peer):
        return remote(pert_ref, pert_all.at[1, m], z_send.at[peer], z_recv.at[m], (s, peer))

    def from_z(peer):
        return remote(pert_ref, pert_all.at[1, peer], z_send.at[m], z_recv.at[peer], (s, peer))

    def near(side, owner, src):
        target = right if side == 0 else left
        return remote(
            src, pert_all.at[2 * side, owner], near_send.at[side, owner],
            near_recv.at[side, owner], (target, m),
        )

    def info(side):
        target = right if side == 0 else left
        return remote(
            extra_ref, extra_all.at[2 * side], info_send.at[side], info_recv.at[side], (target, m)
        )

    order = sorted(range(nm - 1), key=lambda k: abs(k + 1 - nm / 2))
    for k in order:
        to_z(z_peers[k]).start()
    for side in range(2):
        near(side, m, pert_ref).start()
        info(side).start()
    pert_all[1, m] = pert_ref[...]
    extra_all[1] = extra_ref[...]
    loc_f32[...] = loc_ref[...].astype(jnp.float32)

    his = dense.shape[1]
    lobs = lists_ref.shape[1]
    hi_iota = lax.broadcasted_iota(jnp.int32, (his, lobs), 0)
    lo_iota = lax.broadcasted_iota(jnp.int32, (LANES, lobs), 0)
    rows = lax.broadcasted_iota(jnp.int32, (members, LANES), 0)
    cols = lax.broadcasted_iota(jnp.int32, (members, LANES), 1)
    on_diag = rows == cols
    half3 = jnp.where(on_diag, 1.5, 0.0)
    per = CHUNK // LANES

    def spread_lists(first):
        for b in range(group):
            row = send_ref[m, first + b] + m * group_len
            spots = lists_ref[pl.ds(row, 1), :]
            taper = loc_f32[pl.ds(row, 1), :]
            high, low = lax.shift_right_logical(spots, 7), jnp.bitwise_and(spots, LANES - 1)
            hi_hot = jnp.where(hi_iota == high, taper, 0.0).astype(jnp.bfloat16)
            lo_hot = jnp.where(lo_iota == low, 1.0, 0.0).astype(jnp.bfloat16)
            dense[b] = lax.dot_general(
                hi_hot, lo_hot, (((1,), (1,)), ((), ())), preferred_element_type=jnp.float32
            )
        gram[...] = jnp.zeros_like(gram)

    def add_piece(piece):
        def chunk_step(c, carry):
            span = pl.ds(pl.multiple_of(c * CHUNK, CHUNK), CHUNK)
            wide = jnp.concatenate(
                [pert_all[piece, i, :, span].astype(jnp.float32) for i in range(nm)], axis=0
            )
            extra = extra_all[piece, :, span]
            cells = jnp.concatenate([wide.astype(jnp.bfloat16), extra], axis=0)
            wide = wide * extra.astype(jnp.float32)[1:2]
            contract = (((1,), (1,)), ((), ()))
            for b in range(group):
                parts = []
                for j in range(per):
                    weight = dense[b, pl.ds(piece * tile_his + c * per + j, 1), :]
                    parts.append(wide[:, j * LANES : (j + 1) * LANES] * weight)
                high, low = split(jnp.concatenate(parts, axis=1))
                gram[b, :, : cells.shape[0]] += lax.dot_general(
                    high, cells, contract, preferred_element_type=jnp.float32
                ) + lax.dot_general(low, cells, contract, preferred_element_type=jnp.float32)
            return carry

        lax.fori_loop(0, tile_obs // CHUNK, chunk_step, 0)

    def roots_and_weights(first):
        for b in range(group):
            both = gram[b]
            pulled[b] = jnp.sum(jnp.where(cols == members, both, 0.0), axis=1, keepdims=True)
            matrix = jnp.where(cols < members, both, 0.0) + jnp.where(on_diag, members - 1.0, 0.0)
            scale = jnp.sum(
                jnp.sum(jnp.where(on_diag, matrix, 0.0), axis=1, keepdims=True),
                axis=0, keepdims=True,
            )
            scales[b] = jnp.broadcast_to(scale, (1, LANES))
            start = matrix / scale
            correction = half3 - 0.5 * start
            root[b] = halves(mm(left_side(start), right_side(correction)))
            inverse[b] = correction

        def newton(step, carry):
            corrections, pairs = [], []
            filler = jnp.zeros((LANES - members, 2 * LANES), jnp.bfloat16)
            for b in range(group):
                r, z = left_side(root[b]), left_side(inverse[b])
                rhs = jnp.concatenate([r, filler, r, filler], axis=0)
                corrections.append(half3 - 0.5 * halves(mm(z, rhs)))
                pairs.append(jnp.concatenate([r, z], axis=0))
            for b in range(group):
                both = halves(mm(pairs[b], right_side(corrections[b])))
                root[b] = both[:members]
                inverse[b] = both[members:]
            return carry

        lax.fori_loop(0, ITERS - 1, newton, 0)
        for b in range(group):
            z = inverse[b]
            scale = scales[b]
            half_way = jnp.sum(z * pulled[b], axis=0, keepdims=True)
            mean_weight = jnp.sum(z * half_way, axis=1, keepdims=True) / scale[:, :1]
            trans = jnp.sqrt((members - 1.0) / scale) * z + mean_weight
            trans_out[first + b] = trans.astype(jnp.bfloat16)

    spread_lists(0)
    for k in order:
        peer = z_peers[k]
        from_z(peer).wait_recv()
        for side in range(2):
            near(side, peer, pert_all.at[1, peer]).start()
    add_piece(1)
    for side in range(2):
        info(side).wait()
        for i in range(nm):
            near(side, i, pert_all.at[1, i]).wait()
        add_piece(2 * side)
    for peer in z_peers:
        to_z(peer).wait_send()
    roots_and_weights(0)
    if ns > group:

        def more(g, carry):
            spread_lists(g * group)
            for piece in range(3):
                add_piece(piece)
            roots_and_weights(g * group)
            return carry

        lax.fori_loop(1, ns // group, more, 0)

    def to_tile(peer):
        return remote(trans_out.at[peer], trans_in.at[s], t_send.at[peer], t_recv.at[s], (peer, m))

    def from_tile(peer):
        return remote(trans_out.at[peer], trans_in.at[peer], t_send.at[peer], t_recv.at[peer], (peer, m))

    for peer in s_peers:
        to_tile(peer).start()
    trans_in[s] = trans_out[s]
    for peer in s_peers:
        from_tile(peer).wait_recv()

    def mix(o, carry):
        total = jnp.zeros((members, LANES), jnp.float32)
        for i in range(ns):
            total += coef_ref[o, m * ns + i] * trans_in[i].astype(jnp.float32)
        mixed[o] = total
        return carry

    def up(o):
        return remote(
            up_out.at[o], up_in.at[o], up_send.at[o], up_recv.at[o], (s, lax.rem(m + 1, nm))
        )

    def down(o):
        return remote(
            down_out.at[o], down_in.at[o], down_send.at[o], down_recv.at[o],
            (s, lax.rem(m + nm - 1, nm)),
        )

    def first_hop(o, carry):
        mix(o, carry)

        @pl.when(m == 0)
        def _():
            up_out[o] = mixed[o].astype(jnp.bfloat16)
            up(o).start()

        @pl.when(m == nm - 1)
        def _():
            down_out[o] = mixed[o].astype(jnp.bfloat16)
            down(o).start()

        return carry

    lax.fori_loop(0, oblocks, first_hop, 0)

    def later_hops(o, carry):
        @pl.when(m > 0)
        def _():
            up(o).wait_recv()

        @pl.when(jnp.logical_and(m > 0, m < nm - 1))
        def _():
            up_out[o] = (mixed[o] + up_in[o].astype(jnp.float32)).astype(jnp.bfloat16)
            up(o).start()

        @pl.when(m < nm - 1)
        def _():
            down(o).wait_recv()

        @pl.when(jnp.logical_and(m > 0, m < nm - 1))
        def _():
            down_out[o] = (mixed[o] + down_in[o].astype(jnp.float32)).astype(jnp.bfloat16)
            down(o).start()

        @pl.when(m == 0)
        def _():
            out_ref[o] = (mixed[o] + down_in[o].astype(jnp.float32)).astype(jnp.bfloat16)

        @pl.when(m == nm - 1)
        def _():
            out_ref[o] = (mixed[o] + up_in[o].astype(jnp.float32)).astype(jnp.bfloat16)

        @pl.when(jnp.logical_and(m > 0, m < nm - 1))
        def _():
            both = up_in[o].astype(jnp.float32) + down_in[o].astype(jnp.float32)
            out_ref[o] = (mixed[o] + both).astype(jnp.bfloat16)

        return carry

    lax.fori_loop(0, oblocks, later_hops, 0)

    def drain(o, carry):
        @pl.when(m < nm - 1)
        def _():
            up(o).wait_send()

        @pl.when(m > 0)
        def _():
            down(o).wait_send()

        return carry

    lax.fori_loop(0, oblocks, drain, 0)
    for peer in s_peers:
        to_tile(peer).wait_send()


def mixed_weights(send, coef, lists, loc, pert, extra):
    ns, nm = lax.axis_size("space"), lax.axis_size("member")
    shard, tile_obs = pert.shape
    members = shard * nm
    group = 8 if ns % 8 == 0 else ns
    oblocks = coef.shape[0]
    his = 3 * tile_obs // LANES
    vmem = pl.BlockSpec(memory_space=pltpu.VMEM)
    smem = pl.BlockSpec(memory_space=pltpu.SMEM)
    dma = pltpu.SemaphoreType.DMA
    blocks = lambda n, kind: pltpu.VMEM((n, members, LANES), kind)
    return pl.pallas_call(
        functools.partial(letkf_kernel, group, ns, nm),
        in_specs=[smem, smem, vmem, vmem, vmem, vmem],
        out_specs=vmem,
        out_shape=jax.ShapeDtypeStruct((oblocks, members, LANES), jnp.bfloat16),
        scratch_shapes=[
            pltpu.VMEM((3, nm, shard, tile_obs), jnp.bfloat16),
            pltpu.VMEM((3,) + extra.shape, jnp.bfloat16),
            pltpu.VMEM(loc.shape, jnp.float32),
            pltpu.VMEM((group, his, LANES), jnp.float32),
            blocks(group, jnp.float32),
            blocks(group, jnp.float32),
            blocks(group, jnp.float32),
            pltpu.VMEM((group, members, 1), jnp.float32),
            pltpu.VMEM((group, 1, LANES), jnp.float32),
            blocks(ns, jnp.bfloat16),
            blocks(ns, jnp.bfloat16),
            blocks(oblocks, jnp.bfloat16),
            blocks(oblocks, jnp.bfloat16),
            blocks(oblocks, jnp.bfloat16),
            blocks(oblocks, jnp.bfloat16),
            blocks(oblocks, jnp.float32),
            dma((nm,)), dma((nm,)), dma((2, nm)), dma((2, nm)), dma((2,)), dma((2,)),
            dma((ns,)), dma((ns,)),
            dma((oblocks,)), dma((oblocks,)), dma((oblocks,)), dma((oblocks,)),
        ],
        compiler_params=pltpu.CompilerParams(collective_id=0, has_side_effects=True),
        name="mixed_weights",
    )(send, coef, lists, loc, pert, extra)


def apply_weights(ensemble, mixed):
    ens_mean = jnp.mean(ensemble, axis=0, dtype=jnp.float32)
    deviation = (ensemble.astype(jnp.float32) - ens_mean[None]).astype(jnp.bfloat16)
    product = jnp.einsum("jol,oji->iol", deviation, mixed, preferred_element_type=jnp.float32)
    return (ens_mean[None] + product).astype(jnp.bfloat16)


def shards(
    obs_pert,
    innovation,
    obs_prec,
    obs_lists,
    loc_weight,
    send_rows,
    ocean_src,
    ocean_frac,
    ocean_ens,
):
    tile_obs = obs_pert.shape[1]
    extra = jnp.zeros((16, tile_obs), jnp.bfloat16).at[0].set(innovation).at[1].set(obs_prec)
    slots = jnp.arange(lax.axis_size("space") * lax.axis_size("member"), dtype=jnp.int32)[None]
    frac = ocean_frac[:, None]
    coef = jnp.where(ocean_src[:, :1] == slots, 1.0 - frac, 0.0) + jnp.where(
        ocean_src[:, 1:] == slots, frac, 0.0
    )
    mixed = mixed_weights(send_rows[0], coef, obs_lists, loc_weight, obs_pert, extra)
    mixed = mixed[:, :, : ocean_ens.shape[0]]
    return apply_weights(ocean_ens, mixed)


def solution(mesh):
    return jax.shard_map(
        shards,
        mesh=mesh,
        in_specs=(
            P("member", "space"),
            P("space"),
            P("space"),
            P("space", None),
            P("space", None),
            P("space", None, None),
            P("space", None),
            P("space"),
            P(None, "space", "member"),
        ),
        out_specs=P(None, "space", "member"),
        check_vma=False,
    )
```

time: 76.6 us -> 83.4 us (1.089)
  Pallas kernels: 16.7 us -> 76.4 us
  blocking collectives: 34.8 us -> 0 us
  waiting for transfers between devices: 13.5 us -> 0 us
  starting transfers between devices: 6.75 us -> 0 us
  other arithmetic: 0.17 us -> 1.85 us
    pallas_call x1, Pallas kernels: 16.7 us -> 76.4 us  [mixed_weights(): pl.pallas_call(functools.partial(letkf_kernel, group, ns, nm), in_specs=[...]
    all_gather x2 -> x0, blocking collectives: 34.8 us -> none  [the longest x1 18.4 us: shards(): weight_table = lax.all_gather(arrived, 'member', axis=0, tiled=True)]
    ppermute x2 -> x0, waiting for transfers between devices: 7.69 us -> none  [shift(): lax.ppermute(cells, 'space', [(i, (i + by) % count) for i in range(count)])]
    all_to_all x1 -> x0, waiting for transfers between devices: 5.84 us -> none  [shards(): lax.all_to_all(weights, 'space', split_axis=0, concat_axis=0, tiled=True)]
    all_to_all x1 -> x0, starting transfers between devices: 4.06 us -> none  [shards(): lax.all_to_all(weights, 'space', split_axis=0, concat_axis=0, tiled=True)]
    ppermute x2 -> x0, starting transfers between devices: 2.69 us -> none  [shift(): lax.ppermute(cells, 'space', [(i, (i + by) % count) for i in range(count)])]
    unnamed x15 -> x12, local copies, waits for them, and re-layouts: 0.11 us -> 2.66 us
    gather x2 -> x0, local copies, waits for them, and re-layouts: 1.14 us -> none  [the longest x1 0.57 us: shards(): weight_table[ocean_src[:, 1]]]
  transfers between devices with their start and end apart: 3 -> 0, of which waited for: 2 -> 0; matrix products, arithmetic and copies ran while one was open for 0% -> 0% of each run, Pallas kernels for 0% -> 0%
where the time goes in v2:
time: 83.4 us; the launch traced here: 83.2 us
  Pallas kernels  76.4 us (92%)
  local copies, waits for them, and re-layouts  2.81 us (3%)
  matrix products  2.02 us (2%)
  other arithmetic  1.85 us (2%)
    pallas_call x1, Pallas kernels, mixed_weights(): pl.pallas_call(functools.partial(letkf_kernel, group, ns, nm), in_specs=[...  76.4 us
    unnamed x12, local copies, waits for them, and re-layouts  2.66 us
    dot_general x1, matrix products, apply_weights(): jnp.einsum('jol,oji->iol', deviation, mixed, preferred_element_type=jnp.f...  2.02 us

profile of v2, /device:TPU:0, one launch (start us, length us, event | category | flops | bytes accessed | tf_op | source)
XLA Modules:
  0.0 83.2 jit_solution(5098742347232836612)
XLA Ops:
  0.0 0.0 copy-start.5
  0.0 0.7 copy-done.5
  0.7 0.0 copy-start.4
  0.7 0.7 copy-done.4
  1.3 0.0 copy-start.2
  1.3 0.7 select_add_fusion.coef_ref
  2.0 0.0 copy-done.2
  2.0 0.0 copy-start.3
  2.0 0.7 copy-done.3
  2.7 0.0 copy-start
  2.7 1.2 %convert_reduce_fusion = f32[6,512]{1,0:T(8,128)S(1)} fusion(bf16[80,6,512]{2,0,1:T(8,128)(2,1)} %param.21), kind=kLoop, calls=%fused_computation.3 | loop fusion | flops 488448 | bytes 503808 | tf_op jit(solution)/shard_map/reduce_sum | solution.py:356
  3.9 0.1 scatter.9.extra_ref
  4.1 0.0 copy-start.1
  4.1 0.6 copy-done.1
  4.7 76.4 %mixed_weights.1 = bf16[6,80,128]{2,1,0:T(8,128)(2,1)} custom-call(s32[4,8]{1,0:T(4,128)} %bitcast.7, f32[6,32]{1,0:T(8,128)} %select_add_fusion.coef_ref, s32[192,256]{1,0:T(8,128)} %lists_ref.1, bf16[192,256]{1,0:T(8,128)(2,1)} %loc_ref.1, bf16[20,2048]{1,0:T(8,128)(2,1)} %pert_ref.1, bf16[16,2048]{1,0:T(8,128)(2,1)} %copy-done.1), custom_call_target="tpu_custom_call" | custom-call | tf_op jit(solution)/shard_map/mixed_weights/pallas_call | solution.py:324
  81.1 0.0 copy-done
  81.2 2.0 %fusion.1 = bf16[80,6,512]{2,0,1:T(8,128)(2,1)} fusion(bf16[80,6,512]{2,0,1:T(8,128)(2,1)S(1)} %copy-done, f32[6,512]{1,0:T(8,128)S(1)} %broadcast_multiply_fusion, bf16[6,80,128]{2,1,0:T(8,128)(2,1)} %mixed_weights.1), kind=kOutput, calls=%fused_computation.4 | convolution fusion | flops 40550400 | bytes 1138688 | tf_op jit(solution)/shard_map/jol,oji->iol/dot_general | solution.py:358
  (6 shorter events, 0.0 us)
Async XLA Ops:
  0.0 0.7 copy-start.5
  0.7 0.7 copy-start.4
  1.3 0.7 copy-start.2
  2.0 0.7 copy-start.3
  2.7 78.4 %copy-start = (bf16[80,6,512]{2,0,1:T(8,128)(2,1)S(1)}, bf16[80,6,512]{2,0,1:T(8,128)(2,1)}, u32[]{:S(2)}) copy-start(bf16[80,6,512]{2,0,1:T(8,128)(2,1)} %param.21) | copy-start | bytes 1474564
  4.1 0.6 copy-start.1

commit v3 on v2

--- a/solution.py
+++ b/solution.py
@@ -48,8 +48,8 @@
 
 def letkf_kernel(
     group, ns, nm,
-    send_ref, coef_ref, lists_ref, loc_ref, pert_ref, extra_ref, out_ref,
-    pert_all, extra_all, loc_f32, dense, gram, root, inverse, pulled, scales,
+    send_ref, coef_ref, lists_hbm, loc_hbm, pert_ref, extra_ref, out_ref,
+    lists_ref, loc_ref, local_sem, pert_all, extra_all, loc_f32, dense, gram, root, inverse, pulled, scales,
     trans_out, trans_in, up_out, up_in, down_out, down_in, mixed,
     z_send, z_recv, near_send, near_recv, info_send, info_recv, t_send, t_recv,
     up_send, up_recv, down_send, down_recv,
@@ -60,6 +60,11 @@
     tile_obs = pert_ref.shape[1]
     tile_his = tile_obs // LANES
     group_len = lists_ref.shape[0] // nm
+    take_lists = pltpu.make_async_copy(lists_hbm, lists_ref, local_sem.at[0])
+    take_loc = pltpu.make_async_copy(loc_hbm, loc_ref, local_sem.at[1])
+    take_pert = pltpu.make_async_copy(pert_ref, pert_all.at[1, m], local_sem.at[2])
+    for copy in (take_lists, take_loc, take_pert):
+        copy.start()
     oblocks = out_ref.shape[0]
     z_peers = [lax.rem(m + k, nm) for k in range(1, nm)]
     s_peers = [lax.rem(s + k, ns) for k in range(1, ns)]
@@ -97,8 +102,10 @@
     for side in range(2):
         near(side, m, pert_ref).start()
         info(side).start()
-    pert_all[1, m] = pert_ref[...]
     extra_all[1] = extra_ref[...]
+    take_lists.wait()
+    take_loc.wait()
+    take_pert.wait()
     loc_f32[...] = loc_ref[...].astype(jnp.float32)
 
     his = dense.shape[1]
@@ -258,25 +265,41 @@
 
     lax.fori_loop(0, oblocks, first_hop, 0)
 
-    def later_hops(o, carry):
-        @pl.when(m > 0)
-        def _():
-            up(o).wait_recv()
-
-        @pl.when(jnp.logical_and(m > 0, m < nm - 1))
+    def pass_up(o, carry):
+        up(o).wait_recv()
+
+        @pl.when(m < nm - 1)
         def _():
             up_out[o] = (mixed[o] + up_in[o].astype(jnp.float32)).astype(jnp.bfloat16)
             up(o).start()
 
-        @pl.when(m < nm - 1)
-        def _():
-            down(o).wait_recv()
-
-        @pl.when(jnp.logical_and(m > 0, m < nm - 1))
+        return carry
+
+    def pass_down(o, carry):
+        down(o).wait_recv()
+
+        @pl.when(m > 0)
         def _():
             down_out[o] = (mixed[o] + down_in[o].astype(jnp.float32)).astype(jnp.bfloat16)
             down(o).start()
 
+        return carry
+
+    lower = m < nm // 2
+
+    @pl.when(jnp.logical_and(lower, m > 0))
+    def _():
+        lax.fori_loop(0, oblocks, pass_up, 0)
+
+    @pl.when(m < nm - 1)
+    def _():
+        lax.fori_loop(0, oblocks, pass_down, 0)
+
+    @pl.when(jnp.logical_not(lower))
+    def _():
+        lax.fori_loop(0, oblocks, pass_up, 0)
+
+    def finish(o, carry):
         @pl.when(m == 0)
         def _():
             out_ref[o] = (mixed[o] + down_in[o].astype(jnp.float32)).astype(jnp.bfloat16)
@@ -292,7 +315,7 @@
 
         return carry
 
-    lax.fori_loop(0, oblocks, later_hops, 0)
+    lax.fori_loop(0, oblocks, finish, 0)
 
     def drain(o, carry):
         @pl.when(m < nm - 1)
@@ -318,15 +341,19 @@
     oblocks = coef.shape[0]
     his = 3 * tile_obs // LANES
     vmem = pl.BlockSpec(memory_space=pltpu.VMEM)
+    hbm = pl.BlockSpec(memory_space=pl.ANY)
     smem = pl.BlockSpec(memory_space=pltpu.SMEM)
     dma = pltpu.SemaphoreType.DMA
     blocks = lambda n, kind: pltpu.VMEM((n, members, LANES), kind)
     return pl.pallas_call(
         functools.partial(letkf_kernel, group, ns, nm),
-        in_specs=[smem, smem, vmem, vmem, vmem, vmem],
+        in_specs=[smem, smem, hbm, hbm, hbm, vmem],
         out_specs=vmem,
         out_shape=jax.ShapeDtypeStruct((oblocks, members, LANES), jnp.bfloat16),
         scratch_shapes=[
+            pltpu.VMEM(lists.shape, lists.dtype),
+            pltpu.VMEM(loc.shape, loc.dtype),
+            dma((3,)),
             pltpu.VMEM((3, nm, shard, tile_obs), jnp.bfloat16),
             pltpu.VMEM((3,) + extra.shape, jnp.bfloat16),
             pltpu.VMEM(loc.shape, jnp.float32),

time: 83.4 us -> 52.8 us (0.63)
  Pallas kernels: 76.4 us -> 45.8 us
    pallas_call x1, Pallas kernels: 76.4 us -> 45.8 us  [mixed_weights(): pl.pallas_call(functools.partial(letkf_kernel, group, ns, nm), in_specs=[...]
where the time goes in v3:
time: 52.8 us; the launch traced here: 52.6 us
  Pallas kernels  45.8 us (87%)
  local copies, waits for them, and re-layouts  2.81 us (5%)
  matrix products  2.02 us (4%)
  other arithmetic  1.85 us (4%)
    pallas_call x1, Pallas kernels, mixed_weights(): pl.pallas_call(functools.partial(letkf_kernel, group, ns, nm), in_specs=[...  45.8 us
    unnamed x12, local copies, waits for them, and re-layouts  2.66 us
    dot_general x1, matrix products, apply_weights(): jnp.einsum('jol,oji->iol', deviation, mixed, preferred_element_type=jnp.f...  2.02 us
    reduce_sum x1, other arithmetic, apply_weights(): ens_mean = jnp.mean(ensemble, axis=0, dtype=jnp.float32)  1.18 us

profile of v3, /device:TPU:0, one launch (start us, length us, event | category | flops | bytes accessed | tf_op | source)
XLA Modules:
  0.0 52.6 jit_solution(17056511863302529763)
XLA Ops:
  0.0 0.0 copy-start.5
  0.0 0.7 %copy-done.5 = f32[6]{0:T(128)S(1)} copy-done((f32[6]{0:T(128)S(1)}, f32[6]{0:T(128)}, u32[]{:S(2)}) %copy-start.5) | copy-done | bytes 48
  0.7 0.0 copy-start.4
  0.7 0.7 %copy-done.4 = s32[6,2]{0,1:T(2,128)S(1)} copy-done((s32[6,2]{0,1:T(2,128)S(1)}, s32[6,2]{0,1:T(2,128)}, u32[]{:S(2)}) %copy-start.4) | copy-done | bytes 72
  1.3 0.0 copy-start.2
  1.3 0.7 %select_add_fusion.coef_ref = f32[6,32]{1,0:T(8,128)} fusion(f32[6]{0:T(128)S(1)} %copy-done.5, s32[6]{0:T(128)S(1)} %get-tuple-element.30, f32[6]{0:T(128)S(1)} %broadcast_subtract_fusion, s32[6]{0:T(128)S(1)} %get-tuple-element.29), kind=kLoop, calls=%fused_computation.9 | loop fusion | flops 960 | bytes 864 | tf_op jit(solution)/shard_map/add | solution.py:404
  2.0 0.0 copy-done.2
  2.0 0.0 copy-start.3
  2.0 0.7 %copy-done.3 = bf16[2048]{0:T(1024)(128)(2,1)S(1)} copy-done((bf16[2048]{0:T(1024)(128)(2,1)S(1)}, bf16[2048]{0:T(1024)(128)(2,1)}, u32[]{:S(2)}) %copy-start.3) | copy-done | bytes 4120
  2.7 0.0 copy-start
  2.7 1.2 %convert_reduce_fusion = f32[6,512]{1,0:T(8,128)S(1)} fusion(bf16[80,6,512]{2,0,1:T(8,128)(2,1)} %param.21), kind=kLoop, calls=%fused_computation.3 | loop fusion | flops 488448 | bytes 503808 | tf_op jit(solution)/shard_map/reduce_sum | solution.py:383
  3.9 0.1 scatter.9.extra_ref
  4.1 0.0 copy-start.1
  4.1 0.6 %copy-done.1 = bf16[16,2048]{1,0:T(8,128)(2,1)} copy-done((bf16[16,2048]{1,0:T(8,128)(2,1)}, bf16[16,2048]{1,0:T(8,128)(2,1)S(1)}, u32[]{:S(2)}) %copy-start.1) | copy-done | bytes 65560
  4.7 45.8 %mixed_weights.1 = bf16[6,80,128]{2,1,0:T(8,128)(2,1)} custom-call(s32[4,8]{1,0:T(4,128)} %bitcast.7, f32[6,32]{1,0:T(8,128)} %select_add_fusion.coef_ref, s32[192,256]{1,0:T(8,128)} %lists_hbm.1, bf16[192,256]{1,0:T(8,128)(2,1)} %loc_hbm.1, bf16[20,2048]{1,0:T(8,128)(2,1)} %pert_ref.1, bf16[16,2048]{1,0:T(8,128)(2,1)} %copy-done.1), custom_call_target="tpu_custom_call" | custom-call | tf_op jit(solution)/shard_map/mixed_weights/pallas_call | solution.py:348
  50.5 0.0 copy-done
  50.5 2.0 %fusion.1 = bf16[80,6,512]{2,0,1:T(8,128)(2,1)} fusion(bf16[80,6,512]{2,0,1:T(8,128)(2,1)S(1)} %copy-done, f32[6,512]{1,0:T(8,128)S(1)} %broadcast_multiply_fusion, bf16[6,80,128]{2,1,0:T(8,128)(2,1)} %mixed_weights.1), kind=kOutput, calls=%fused_computation.4 | convolution fusion | flops 40550400 | bytes 1138688 | tf_op jit(solution)/shard_map/jol,oji->iol/dot_general | solution.py:385
  (6 shorter events, 0.0 us)
Async XLA Ops:
  0.0 0.7 %copy-start.5 = (f32[6]{0:T(128)S(1)}, f32[6]{0:T(128)}, u32[]{:S(2)}) copy-start(f32[6]{0:T(128)} %param.20) | copy-start | bytes 76
  0.7 0.7 %copy-start.4 = (s32[6,2]{0,1:T(2,128)S(1)}, s32[6,2]{0,1:T(2,128)}, u32[]{:S(2)}) copy-start(s32[6,2]{0,1:T(2,128)} %param.19) | copy-start | bytes 148
  1.3 0.7 %copy-start.2 = (bf16[2048]{0:T(1024)(128)(2,1)S(1)}, bf16[2048]{0:T(1024)(128)(2,1)}, u32[]{:S(2)}) copy-start(bf16[2048]{0:T(1024)(128)(2,1)} %param.14) | copy-start | bytes 12292
  2.0 0.7 %copy-start.3 = (bf16[2048]{0:T(1024)(128)(2,1)S(1)}, bf16[2048]{0:T(1024)(128)(2,1)}, u32[]{:S(2)}) copy-start(bf16[2048]{0:T(1024)(128)(2,1)} %param.15) | copy-start | bytes 12292
  2.7 47.8 %copy-start = (bf16[80,6,512]{2,0,1:T(8,128)(2,1)S(1)}, bf16[80,6,512]{2,0,1:T(8,128)(2,1)}, u32[]{:S(2)}) copy-start(bf16[80,6,512]{2,0,1:T(8,128)(2,1)} %param.21) | copy-start | bytes 1474564
  4.1 0.6 %copy-start.1 = (bf16[16,2048]{1,0:T(8,128)(2,1)}, bf16[16,2048]{1,0:T(8,128)(2,1)S(1)}, u32[]{:S(2)}) copy-start(bf16[16,2048]{1,0:T(8,128)(2,1)S(1)} %scatter.9.extra_ref) | copy-start | bytes 196612

commit v4 on v3

--- a/solution.py
+++ b/solution.py
@@ -48,7 +48,7 @@
 
 def letkf_kernel(
     group, ns, nm,
-    send_ref, coef_ref, lists_hbm, loc_hbm, pert_ref, extra_ref, out_ref,
+    send_ref, src_ref, frac_ref, lists_hbm, loc_hbm, pert_ref, extra_ref, out_ref,
     lists_ref, loc_ref, local_sem, pert_all, extra_all, loc_f32, dense, gram, root, inverse, pulled, scales,
     trans_out, trans_in, up_out, up_in, down_out, down_in, mixed,
     z_send, z_recv, near_send, near_recv, info_send, info_recv, t_send, t_recv,
@@ -232,8 +232,11 @@
 
     def mix(o, carry):
         total = jnp.zeros((members, LANES), jnp.float32)
+        one, two, frac = src_ref[o, 0], src_ref[o, 1], frac_ref[o]
         for i in range(ns):
-            total += coef_ref[o, m * ns + i] * trans_in[i].astype(jnp.float32)
+            slot = m * ns + i
+            weight = jnp.where(one == slot, 1.0 - frac, 0.0) + jnp.where(two == slot, frac, 0.0)
+            total += weight * trans_in[i].astype(jnp.float32)
         mixed[o] = total
         return carry
 
@@ -333,12 +336,12 @@
         to_tile(peer).wait_send()
 
 
-def mixed_weights(send, coef, lists, loc, pert, extra):
+def mixed_weights(send, src, frac, lists, loc, pert, extra):
     ns, nm = lax.axis_size("space"), lax.axis_size("member")
     shard, tile_obs = pert.shape
     members = shard * nm
     group = 8 if ns % 8 == 0 else ns
-    oblocks = coef.shape[0]
+    oblocks = src.shape[0]
     his = 3 * tile_obs // LANES
     vmem = pl.BlockSpec(memory_space=pltpu.VMEM)
     hbm = pl.BlockSpec(memory_space=pl.ANY)
@@ -347,7 +350,7 @@
     blocks = lambda n, kind: pltpu.VMEM((n, members, LANES), kind)
     return pl.pallas_call(
         functools.partial(letkf_kernel, group, ns, nm),
-        in_specs=[smem, smem, hbm, hbm, hbm, vmem],
+        in_specs=[smem, smem, smem, hbm, hbm, hbm, vmem],
         out_specs=vmem,
         out_shape=jax.ShapeDtypeStruct((oblocks, members, LANES), jnp.bfloat16),
         scratch_shapes=[
@@ -376,7 +379,7 @@
         ],
         compiler_params=pltpu.CompilerParams(collective_id=0, has_side_effects=True),
         name="mixed_weights",
-    )(send, coef, lists, loc, pert, extra)
+    )(send, src, frac, lists, loc, pert, extra)
 
 
 def apply_weights(ensemble, mixed):
@@ -399,12 +402,9 @@
 ):
     tile_obs = obs_pert.shape[1]
     extra = jnp.zeros((16, tile_obs), jnp.bfloat16).at[0].set(innovation).at[1].set(obs_prec)
-    slots = jnp.arange(lax.axis_size("space") * lax.axis_size("member"), dtype=jnp.int32)[None]
-    frac = ocean_frac[:, None]
-    coef = jnp.where(ocean_src[:, :1] == slots, 1.0 - frac, 0.0) + jnp.where(
-        ocean_src[:, 1:] == slots, frac, 0.0
+    mixed = mixed_weights(
+        send_rows[0], ocean_src, ocean_frac, obs_lists, loc_weight, obs_pert, extra
     )
-    mixed = mixed_weights(send_rows[0], coef, obs_lists, loc_weight, obs_pert, extra)
     mixed = mixed[:, :, : ocean_ens.shape[0]]
     return apply_weights(ocean_ens, mixed)
 

time: 52.8 us -> 52.2 us (0.989)
  other arithmetic: 1.85 us -> 1.19 us
    add x1 -> x0, other arithmetic: 0.66 us -> none  [shards(): jnp.where(ocean_src[:, :1] == slots, 1.0 - frac, 0.0)]
    unnamed x12 -> x11, local copies, waits for them, and re-layouts: 2.66 us -> 2.66 us
where the time goes in v4:
time: 52.2 us; the launch traced here: 51.9 us
  Pallas kernels  45.8 us (88%)
  local copies, waits for them, and re-layouts  2.8 us (5%)
  matrix products  2.02 us (4%)
  other arithmetic  1.19 us (2%)
    pallas_call x1, Pallas kernels, mixed_weights(): pl.pallas_call(functools.partial(letkf_kernel, group, ns, nm), in_specs=[...  45.8 us
    unnamed x11, local copies, waits for them, and re-layouts  2.66 us
    dot_general x1, matrix products, apply_weights(): jnp.einsum('jol,oji->iol', deviation, mixed, preferred_element_type=jnp.f...  2.02 us
    reduce_sum x1, other arithmetic, apply_weights(): ens_mean = jnp.mean(ensemble, axis=0, dtype=jnp.float32)  1.18 us

profile of v4, /device:TPU:0, one launch (start us, length us, event | category | flops | bytes accessed | tf_op | source)
XLA Modules:
  0.0 51.9 jit_solution(18130629942553356644)
XLA Ops:
  0.0 0.0 copy-start.4
  0.0 0.0 copy-start.2
  0.0 0.7 %copy-done.4 = s32[6,2]{0,1:T(2,128)S(1)} copy-done((s32[6,2]{0,1:T(2,128)S(1)}, s32[6,2]{0,1:T(2,128)}, u32[]{:S(2)}) %copy-start.4) | copy-done | bytes 72
  0.7 0.7 %copy.10.src_ref = s32[6,2]{1,0:T(8,128)} copy(s32[6,2]{0,1:T(2,128)S(1)} %copy-done.4) | data formatting | bytes 96 | tf_op args[6]
  1.4 0.0 copy-done.2
  1.4 0.0 copy-start.3
  1.4 0.7 %copy-done.3 = bf16[2048]{0:T(1024)(128)(2,1)S(1)} copy-done((bf16[2048]{0:T(1024)(128)(2,1)S(1)}, bf16[2048]{0:T(1024)(128)(2,1)}, u32[]{:S(2)}) %copy-start.3) | copy-done | bytes 4120
  2.1 0.0 copy-start
  2.1 1.2 %convert_reduce_fusion = f32[6,512]{1,0:T(8,128)S(1)} fusion(bf16[80,6,512]{2,0,1:T(8,128)(2,1)} %param.21), kind=kLoop, calls=%fused_computation.3 | loop fusion | flops 488448 | bytes 503808 | tf_op jit(solution)/shard_map/reduce_sum | solution.py:386
  3.3 0.1 scatter.9.extra_ref
  3.4 0.0 copy-start.1
  3.4 0.6 %copy-done.1 = bf16[16,2048]{1,0:T(8,128)(2,1)} copy-done((bf16[16,2048]{1,0:T(8,128)(2,1)}, bf16[16,2048]{1,0:T(8,128)(2,1)S(1)}, u32[]{:S(2)}) %copy-start.1) | copy-done | bytes 65560
  4.0 45.8 %mixed_weights.1 = bf16[6,80,128]{2,1,0:T(8,128)(2,1)} custom-call(s32[4,8]{1,0:T(4,128)} %bitcast.3, s32[6,2]{1,0:T(8,128)} %copy.10.src_ref, f32[6]{0:T(128)} %frac_ref.1, s32[192,256]{1,0:T(8,128)} %lists_hbm.1, bf16[192,256]{1,0:T(8,128)(2,1)} %loc_hbm.1, bf16[20,2048]{1,0:T(8,128)(2,1)} %pert_ref.1, bf16[16,2048]{1,0:T(8,128)(2,1)} %copy-done.1), custom_call_target="tpu_custom_call" | custom-call | tf_op jit(solution)/shard_map/mixed_weights/pallas_call | solution.py:351
  49.9 0.0 copy-done
  49.9 2.0 %fusion.1 = bf16[80,6,512]{2,0,1:T(8,128)(2,1)} fusion(bf16[80,6,512]{2,0,1:T(8,128)(2,1)S(1)} %copy-done, f32[6,512]{1,0:T(8,128)S(1)} %broadcast_multiply_fusion, bf16[6,80,128]{2,1,0:T(8,128)(2,1)} %mixed_weights.1), kind=kOutput, calls=%fused_computation.4 | convolution fusion | flops 40550400 | bytes 1138688 | tf_op jit(solution)/shard_map/jol,oji->iol/dot_general | solution.py:388
  (4 shorter events, 0.0 us)
Async XLA Ops:
  0.0 0.7 %copy-start.4 = (s32[6,2]{0,1:T(2,128)S(1)}, s32[6,2]{0,1:T(2,128)}, u32[]{:S(2)}) copy-start(s32[6,2]{0,1:T(2,128)} %param.19) | copy-start | bytes 148
  0.0 1.4 %copy-start.2 = (bf16[2048]{0:T(1024)(128)(2,1)S(1)}, bf16[2048]{0:T(1024)(128)(2,1)}, u32[]{:S(2)}) copy-start(bf16[2048]{0:T(1024)(128)(2,1)} %param.14) | copy-start | bytes 12292
  1.4 0.7 %copy-start.3 = (bf16[2048]{0:T(1024)(128)(2,1)S(1)}, bf16[2048]{0:T(1024)(128)(2,1)}, u32[]{:S(2)}) copy-start(bf16[2048]{0:T(1024)(128)(2,1)} %param.15) | copy-start | bytes 12292
  2.1 47.8 %copy-start = (bf16[80,6,512]{2,0,1:T(8,128)(2,1)S(1)}, bf16[80,6,512]{2,0,1:T(8,128)(2,1)}, u32[]{:S(2)}) copy-start(bf16[80,6,512]{2,0,1:T(8,128)(2,1)} %param.21) | copy-start | bytes 1474564
  3.4 0.6 %copy-start.1 = (bf16[16,2048]{1,0:T(8,128)(2,1)}, bf16[16,2048]{1,0:T(8,128)(2,1)S(1)}, u32[]{:S(2)}) copy-start(bf16[16,2048]{1,0:T(8,128)(2,1)S(1)} %scatter.9.extra_ref) | copy-start | bytes 196612

commit v5 on v4

--- a/solution.py
+++ b/solution.py
@@ -232,7 +232,7 @@
 
     def mix(o, carry):
         total = jnp.zeros((members, LANES), jnp.float32)
-        one, two, frac = src_ref[o, 0], src_ref[o, 1], frac_ref[o]
+        one, two, frac = src_ref[0, o], src_ref[1, o], frac_ref[o]
         for i in range(ns):
             slot = m * ns + i
             weight = jnp.where(one == slot, 1.0 - frac, 0.0) + jnp.where(two == slot, frac, 0.0)
@@ -341,7 +341,7 @@
     shard, tile_obs = pert.shape
     members = shard * nm
     group = 8 if ns % 8 == 0 else ns
-    oblocks = src.shape[0]
+    oblocks = src.shape[1]
     his = 3 * tile_obs // LANES
     vmem = pl.BlockSpec(memory_space=pltpu.VMEM)
     hbm = pl.BlockSpec(memory_space=pl.ANY)
@@ -403,7 +403,7 @@
     tile_obs = obs_pert.shape[1]
     extra = jnp.zeros((16, tile_obs), jnp.bfloat16).at[0].set(innovation).at[1].set(obs_prec)
     mixed = mixed_weights(
-        send_rows[0], ocean_src, ocean_frac, obs_lists, loc_weight, obs_pert, extra
+        send_rows[0], ocean_src.T, ocean_frac, obs_lists, loc_weight, obs_pert, extra
     )
     mixed = mixed[:, :, : ocean_ens.shape[0]]
     return apply_weights(ocean_ens, mixed)

time: 52.2 us -> 50.8 us (0.973)
  local copies, waits for them, and re-layouts: 2.8 us -> 1.48 us
    unnamed x11 -> x6, local copies, waits for them, and re-layouts: 2.66 us -> 0.63 us
    another operation x2, local copies, waits for them, and re-layouts: 0.01 us -> 0.71 us
where the time goes in v5:
time: 50.8 us; the launch traced here: 50.6 us
  Pallas kernels  45.8 us (90%)
  matrix products  2.02 us (4%)
  local copies, waits for them, and re-layouts  1.48 us (3%)
  other arithmetic  1.18 us (2%)
    pallas_call x1, Pallas kernels, mixed_weights(): pl.pallas_call(functools.partial(letkf_kernel, group, ns, nm), in_specs=[...  45.8 us
    dot_general x1, matrix products, apply_weights(): jnp.einsum('jol,oji->iol', deviation, mixed, preferred_element_type=jnp.f...  2.02 us
    reduce_sum x1, other arithmetic, apply_weights(): ens_mean = jnp.mean(ensemble, axis=0, dtype=jnp.float32)  1.18 us

profile of v5, /device:TPU:0, one launch (start us, length us, event | category | flops | bytes accessed | tf_op | source)
XLA Modules:
  0.0 50.6 jit_solution(15993530886445570110)
XLA Ops:
  0.0 0.0 copy-start.2
  0.0 0.7 %reshape.55 = bf16[1,2048]{1,0:T(2,128)(2,1)S(1)} reshape(bf16[2048]{0:T(1024)(128)(2,1)} %param.14) | data formatting | bytes 8192 | tf_op jit(solution)/shard_map/reshape.47
  0.7 0.0 copy-done.2
  0.7 0.0 copy-start
  0.7 1.2 %convert_reduce_fusion = f32[6,512]{1,0:T(8,128)S(1)} fusion(bf16[80,6,512]{2,0,1:T(8,128)(2,1)} %param.21), kind=kLoop, calls=%fused_computation.3 | loop fusion | flops 488448 | bytes 503808 | tf_op jit(solution)/shard_map/reduce_sum | solution.py:386
  2.0 0.1 scatter.9.extra_ref
  2.1 0.0 copy-start.1
  2.1 0.6 %copy-done.1 = bf16[16,2048]{1,0:T(8,128)(2,1)} copy-done((bf16[16,2048]{1,0:T(8,128)(2,1)}, bf16[16,2048]{1,0:T(8,128)(2,1)S(1)}, u32[]{:S(2)}) %copy-start.1) | copy-done | bytes 65560
  2.7 45.8 %mixed_weights.1 = bf16[6,80,128]{2,1,0:T(8,128)(2,1)} custom-call(s32[4,8]{1,0:T(4,128)} %bitcast.4, s32[2,6]{1,0:T(2,128)} %bitcast.5, f32[6]{0:T(128)} %frac_ref.1, s32[192,256]{1,0:T(8,128)} %lists_hbm.1, bf16[192,256]{1,0:T(8,128)(2,1)} %loc_hbm.1, bf16[20,2048]{1,0:T(8,128)(2,1)} %pert_ref.1, bf16[16,2048]{1,0:T(8,128)(2,1)} %copy-done.1), custom_call_target="tpu_custom_call" | custom-call | tf_op jit(solution)/shard_map/mixed_weights/pallas_call | solution.py:351
  48.5 0.0 copy-done
  48.6 2.0 %fusion.1 = bf16[80,6,512]{2,0,1:T(8,128)(2,1)} fusion(bf16[80,6,512]{2,0,1:T(8,128)(2,1)S(1)} %copy-done, f32[6,512]{1,0:T(8,128)S(1)} %broadcast_multiply_fusion, bf16[6,80,128]{2,1,0:T(8,128)(2,1)} %mixed_weights.1), kind=kOutput, calls=%fused_computation.4 | convolution fusion | flops 40550400 | bytes 1138688 | tf_op jit(solution)/shard_map/jol,oji->iol/dot_general | solution.py:388
  (3 shorter events, 0.0 us)
Async XLA Ops:
  0.0 0.7 %copy-start.2 = (bf16[2048]{0:T(1024)(128)(2,1)S(1)}, bf16[2048]{0:T(1024)(128)(2,1)}, u32[]{:S(2)}) copy-start(bf16[2048]{0:T(1024)(128)(2,1)} %param.15) | copy-start | bytes 12292
  0.7 47.8 %copy-start = (bf16[80,6,512]{2,0,1:T(8,128)(2,1)S(1)}, bf16[80,6,512]{2,0,1:T(8,128)(2,1)}, u32[]{:S(2)}) copy-start(bf16[80,6,512]{2,0,1:T(8,128)(2,1)} %param.21) | copy-start | bytes 1474564
  2.1 0.6 %copy-start.1 = (bf16[16,2048]{1,0:T(8,128)(2,1)}, bf16[16,2048]{1,0:T(8,128)(2,1)S(1)}, u32[]{:S(2)}) copy-start(bf16[16,2048]{1,0:T(8,128)(2,1)S(1)} %scatter.9.extra_ref) | copy-start | bytes 196612
